TPU v7x, 32 devices: a whole 2x2x4 slice. The times are simulated.
32 devices in a mesh: wide: 8 (over z, x), narrow: 4 (over y, core).
Axes of the slice: x: 2, y: 2, z: 4, core: 2. Of those that a mesh axis runs over, the one named last changes fastest.
Arguments:
- latents: bfloat16 [128, 32, 32, 384], P('wide', 'narrow'), may hold values from -6 to 6
- timesteps: int32 [128], P('wide'), may hold values from 0 to 999
- out_grad: bfloat16 [128, 16, 16, 768], P(('wide', 'narrow')), may hold values from -6 to 6
- ada_weight: bfloat16 [256, 2304], replicated, may hold values from -1 to 1
- ada_bias: bfloat16 [2304], replicated, may hold values from -4 to 4
- conv_attn: bfloat16 [3, 3, 384], replicated, may hold values from -2 to 2
- qkv_weight: bfloat16 [384, 1152], replicated, may hold values from -0.3125 to 0.3125
- proj_weight: bfloat16 [384, 384], replicated, may hold values from -1.25 to 1.25
- fc1_weight: bfloat16 [384, 1536], replicated, may hold values from -0.3125 to 0.3125
- fc1_bias: bfloat16 [1536], replicated, may hold values from -6 to 6
- conv_ffn: bfloat16 [3, 3, 1536], replicated, may hold values from -2 to 2
- fc2_weight: bfloat16 [1536, 384], replicated, may hold values from -0.15625 to 0.15625
- fc2_bias: bfloat16 [384], replicated, may hold values from -4 to 4
- down_weight: bfloat16 [1536, 768], replicated, may hold values from -0.15625 to 0.15625
- down_bias: bfloat16 [768], replicated, may hold values from -4 to 4
Outputs:
- result: bfloat16 [128, 16, 16, 768], P(('wide', 'narrow'))
- grad_latents: float32 [128, 32, 32, 384], P('wide', 'narrow')
- grad_ada_weight: float32 [256, 2304], replicated
- grad_ada_bias: float32 [2304], replicated
- grad_conv_attn: float32 [3, 3, 384], replicated
- grad_qkv_weight: float32 [384, 1152], replicated
- grad_proj_weight: float32 [384, 384], replicated
- grad_fc1_weight: float32 [384, 1536], replicated
- grad_fc1_bias: float32 [1536], replicated
- grad_conv_ffn: float32 [3, 3, 1536], replicated
- grad_fc2_weight: float32 [1536, 384], replicated
- grad_fc2_bias: float32 [384], replicated
- grad_down_weight: float32 [1536, 768], replicated
- grad_down_bias: float32 [768], replicated
All inputs are finite; a program needn't handle non-finite values.
Results may differ from a plain program's by a relative error of at most 0.018.
The roundings to bfloat16 on the way count: a program that leaves them out, or rounds other values in their place, can miss the bound.
Values may be sent and summed in bfloat16 or wider, within the bound.
No kernel may reach another device: no remote copies, remote signals or barrier semaphores. Data moves between devices by JAX's collectives and lax.ppermute only.
A program may use at most 384 MiB of HBM per device.

v0:
```python
import math
import jax
import jax.numpy as jnp
from jax import lax
from jax.sharding import PartitionSpec as P

HEADS = 6
EPSILON = 1e-06
HIGH = lax.Precision.HIGHEST


def with_halo(block, sides, width):
    for axis, dim in sides:
        count = lax.axis_size(axis)
        forward = [(i, i + 1) for i in range(count - 1)]
        backward = [(target, source) for source, target in forward]
        low = lax.ppermute(
            lax.slice_in_dim(block, block.shape[dim] - width, None, axis=dim), axis, forward
        )
        high = lax.ppermute(lax.slice_in_dim(block, 0, width, axis=dim), axis, backward)
        block = jnp.concatenate([low, block, high], axis=dim)
    return block


def timestep_features(steps_in, feature_count):
    half_count = feature_count // 2
    freq_table = jnp.exp(
        -math.log(10000.0) * jnp.arange(half_count, dtype=jnp.float32) / half_count
    )
    angles = steps_in.astype(jnp.float32)[:, None] * freq_table[None, :]
    return jnp.concatenate([jnp.cos(angles), jnp.sin(angles)], axis=1)


def layer_norm(values):
    center = values - jnp.mean(values, axis=-1, keepdims=True)
    spread = jnp.mean(center * center, axis=-1, keepdims=True)
    return center * lax.rsqrt(spread + EPSILON)


def modulate_norm(values, shift_part, scale_part):
    return layer_norm(values) * (1.0 + scale_part) + shift_part


def gelu_tanh(values):
    return jax.nn.gelu(values, approximate=True)


def depth_conv(row_padded, kernel):
    row_count = row_padded.shape[1] - 2
    col_count = row_padded.shape[2]
    padded = jnp.pad(row_padded, ((0, 0), (0, 0), (1, 1), (0, 0)))
    total = jnp.zeros((row_padded.shape[0], row_count, col_count, row_padded.shape[3]), jnp.float32)
    for row_tap in range(3):
        for col_tap in range(3):
            window = padded[
                :, row_tap : row_tap + row_count, col_tap : col_tap + col_count, :
            ].astype(jnp.float32)
            total = total + window * kernel[row_tap, col_tap].astype(jnp.float32)
    return total


def depth_conv_grads(row_padded, grad_padded, kernel):
    row_count = grad_padded.shape[1] - 2
    col_count = grad_padded.shape[2]
    inputs_full = jnp.pad(row_padded, ((0, 0), (0, 0), (1, 1), (0, 0)))
    grads_full = jnp.pad(grad_padded, ((0, 0), (0, 0), (1, 1), (0, 0)))
    centre = grad_padded[:, 1 : 1 + row_count, :, :].astype(jnp.float32)
    input_grad = jnp.zeros(centre.shape, jnp.float32)
    kernel_rows = []
    for row_tap in range(3):
        tap_list = []
        for col_tap in range(3):
            window = inputs_full[
                :, row_tap : row_tap + row_count, col_tap : col_tap + col_count, :
            ].astype(jnp.float32)
            tap_list.append(jnp.sum(window * centre, axis=(0, 1, 2)))
            mirror = grads_full[
                :, 2 - row_tap : 2 - row_tap + row_count, 2 - col_tap : 2 - col_tap + col_count, :
            ].astype(jnp.float32)
            input_grad = input_grad + mirror * kernel[row_tap, col_tap].astype(jnp.float32)
        kernel_rows.append(jnp.stack(tap_list))
    return (jnp.stack(kernel_rows), input_grad)


def to_groups(values, head_count):
    batch_size, row_count, col_count, channels = values.shape
    head_size = channels // head_count
    shaped = values.reshape(batch_size, row_count // 2, 2, col_count // 2, 2, head_count, head_size)
    shaped = shaped.transpose(0, 2, 4, 5, 1, 3, 6)
    return shaped.reshape(batch_size, 4, head_count, row_count // 2 * (col_count // 2), head_size)


def from_groups(values, row_count, col_count):
    batch_size = values.shape[0]
    head_count = values.shape[2]
    head_size = values.shape[4]
    shaped = values.reshape(batch_size, 2, 2, head_count, row_count // 2, col_count // 2, head_size)
    shaped = shaped.transpose(0, 4, 1, 5, 2, 3, 6)
    return shaped.reshape(batch_size, row_count, col_count, head_count * head_size)


def unshuffle(values):
    batch_size, row_count, col_count, channels = values.shape
    shaped = values.reshape(batch_size, row_count // 2, 2, col_count // 2, 2, channels)
    return shaped.transpose(0, 1, 3, 2, 4, 5).reshape(
        batch_size, row_count // 2, col_count // 2, 4 * channels
    )


def shuffle(values):
    batch_size, half_rows, half_cols, wide_channels = values.shape
    channels = wide_channels // 4
    shaped = values.reshape(batch_size, half_rows, half_cols, 2, 2, channels)
    return shaped.transpose(0, 1, 3, 2, 4, 5).reshape(
        batch_size, 2 * half_rows, 2 * half_cols, channels
    )


def attend_scores(q_groups, k_groups):
    factor = q_groups.shape[-1] ** (-0.5)
    return (
        jnp.einsum("bghqe,bghke->bghqk", q_groups, k_groups, preferred_element_type=jnp.float32)
        * factor
    )


def shards(
    latents,
    timesteps,
    out_grad,
    ada_weight,
    ada_bias,
    conv_attn,
    qkv_weight,
    proj_weight,
    fc1_weight,
    fc1_bias,
    conv_ffn,
    fc2_weight,
    fc2_bias,
    down_weight,
    down_bias,
):
    channels = latents.shape[3]
    cond_all = jax.nn.silu(timestep_features(timesteps, ada_weight.shape[0])).astype(jnp.bfloat16)
    mod_all = jnp.dot(cond_all, ada_weight, preferred_element_type=jnp.float32) + ada_bias.astype(
        jnp.float32
    )
    image_count = latents.shape[0]
    row_count = latents.shape[1]
    col_count = latents.shape[2]
    pieces = [
        mod_all[:, None, None, part_index * channels : (part_index + 1) * channels]
        for part_index in range(6)
    ]
    shift_one, scale_one, gate_one, shift_two, scale_two, gate_two = pieces
    values_in = latents.astype(jnp.float32)
    hidden_in = modulate_norm(values_in, shift_one, scale_one).astype(jnp.bfloat16)
    padded_in = with_halo(hidden_in, (("narrow", 1),), 1)
    conv_out = depth_conv(padded_in, conv_attn).astype(jnp.bfloat16)
    qkv_all = jnp.dot(conv_out, qkv_weight, preferred_element_type=jnp.float32)
    query_own = qkv_all[..., :channels].astype(jnp.bfloat16)
    pair_own = qkv_all[..., channels:].astype(jnp.bfloat16)
    pair_all = lax.all_gather(pair_own, "narrow", axis=1, tiled=True)
    key_rows = pair_all.shape[1]
    q_groups = to_groups(query_own, HEADS)
    k_groups = to_groups(pair_all[..., :channels], HEADS)
    v_groups = to_groups(pair_all[..., channels:], HEADS)
    scores = attend_scores(q_groups, k_groups)
    top_score = jnp.max(scores, axis=-1, keepdims=True)
    log_total = top_score + jnp.log(jnp.sum(jnp.exp(scores - top_score), axis=-1, keepdims=True))
    probs_low = jnp.exp(scores - log_total).astype(jnp.bfloat16)
    mixed_groups = jnp.einsum(
        "bghqk,bghke->bghqe", probs_low, v_groups, preferred_element_type=jnp.float32
    )
    mixed = from_groups(mixed_groups, row_count, col_count).astype(jnp.bfloat16)
    attn_out = jnp.dot(mixed, proj_weight, preferred_element_type=jnp.float32)
    after_attn = values_in + gate_one * attn_out
    hidden_two = modulate_norm(after_attn, shift_two, scale_two).astype(jnp.bfloat16)
    ffn_pre = (
        jnp.dot(hidden_two, fc1_weight, preferred_element_type=jnp.float32)
        + fc1_bias.astype(jnp.float32)
    ).astype(jnp.bfloat16)
    padded_ffn = with_halo(ffn_pre, (("narrow", 1),), 1)
    ffn_conv = depth_conv(padded_ffn, conv_ffn)
    activated = gelu_tanh(ffn_conv).astype(jnp.bfloat16)
    ffn_out = jnp.dot(activated, fc2_weight, preferred_element_type=jnp.float32) + fc2_bias.astype(
        jnp.float32
    )
    after_ffn = after_attn + gate_two * ffn_out
    low_res = unshuffle(after_ffn).astype(jnp.bfloat16)
    result_own = (
        jnp.dot(low_res, down_weight, preferred_element_type=jnp.float32)
        + down_bias.astype(jnp.float32)
    ).astype(jnp.bfloat16)
    result = lax.all_to_all(result_own, "narrow", split_axis=0, concat_axis=1, tiled=True)
    grad_low = lax.all_to_all(out_grad, "narrow", split_axis=1, concat_axis=0, tiled=True)
    grad_down_weight = jnp.einsum(
        "bijc,bijo->co", low_res, grad_low, preferred_element_type=jnp.float32
    )
    grad_down_bias = jnp.sum(grad_low.astype(jnp.float32), axis=(0, 1, 2))
    grad_after = shuffle(
        jnp.einsum("bijo,co->bijc", grad_low, down_weight, preferred_element_type=jnp.float32)
    )
    grad_ffn_out = (gate_two * grad_after).astype(jnp.bfloat16)
    grad_gate_two = jnp.sum(ffn_out * grad_after, axis=(1, 2))
    grad_fc2_weight = jnp.einsum(
        "brwf,brwd->fd", activated, grad_ffn_out, preferred_element_type=jnp.float32
    )
    grad_fc2_bias = jnp.sum(grad_ffn_out.astype(jnp.float32), axis=(0, 1, 2))
    grad_act = jnp.einsum(
        "brwd,fd->brwf", grad_ffn_out, fc2_weight, preferred_element_type=jnp.float32
    )
    unused_gelu, gelu_back = jax.vjp(gelu_tanh, ffn_conv)
    grad_conv = gelu_back(grad_act)[0].astype(jnp.bfloat16)
    grad_conv_pad = with_halo(grad_conv, (("narrow", 1),), 1)
    grad_conv_ffn, grad_pre = depth_conv_grads(padded_ffn, grad_conv_pad, conv_ffn)
    grad_pre_low = grad_pre.astype(jnp.bfloat16)
    grad_fc1_weight = jnp.einsum(
        "brwd,brwf->df", hidden_two, grad_pre_low, preferred_element_type=jnp.float32
    )
    grad_fc1_bias = jnp.sum(grad_pre_low.astype(jnp.float32), axis=(0, 1, 2))
    grad_hidden_two = jnp.einsum(
        "brwf,df->brwd", grad_pre_low, fc1_weight, preferred_element_type=jnp.float32
    )
    unused_two, norm_back_two = jax.vjp(modulate_norm, after_attn, shift_two, scale_two)
    grad_from_two, grad_shift_two, grad_scale_two = norm_back_two(grad_hidden_two)
    grad_mid = grad_after + grad_from_two
    grad_attn_out = (gate_one * grad_mid).astype(jnp.bfloat16)
    grad_gate_one = jnp.sum(attn_out * grad_mid, axis=(1, 2))
    grad_proj_weight = jnp.einsum(
        "brwd,brwe->de", mixed, grad_attn_out, preferred_element_type=jnp.float32
    )
    grad_mixed = jnp.einsum(
        "brwe,de->brwd", grad_attn_out, proj_weight, preferred_element_type=jnp.float32
    ).astype(jnp.bfloat16)
    grad_mixed_groups = to_groups(grad_mixed, HEADS)
    scores_again = attend_scores(q_groups, k_groups)
    probs_again = jnp.exp(scores_again - log_total)
    probs_again_low = probs_again.astype(jnp.bfloat16)
    grad_probs = jnp.einsum(
        "bghqe,bghke->bghqk", grad_mixed_groups, v_groups, preferred_element_type=jnp.float32
    )
    grad_value_groups = jnp.einsum(
        "bghqk,bghqe->bghke", probs_again_low, grad_mixed_groups, preferred_element_type=jnp.float32
    )
    inner_sum = jnp.sum(probs_again * grad_probs, axis=-1, keepdims=True)
    grad_scores = (probs_again * (grad_probs - inner_sum)).astype(jnp.bfloat16)
    factor = q_groups.shape[-1] ** (-0.5)
    grad_query_groups = factor * jnp.einsum(
        "bghqk,bghke->bghqe", grad_scores, k_groups, preferred_element_type=jnp.float32
    )
    grad_key_groups = factor * jnp.einsum(
        "bghqk,bghqe->bghke", grad_scores, q_groups, preferred_element_type=jnp.float32
    )
    grad_pair = jnp.concatenate(
        [
            from_groups(grad_key_groups, key_rows, col_count),
            from_groups(grad_value_groups, key_rows, col_count),
        ],
        axis=-1,
    )
    grad_pair_own = lax.psum_scatter(
        grad_pair.astype(jnp.bfloat16), "narrow", scatter_dimension=1, tiled=True
    ).astype(jnp.float32)
    grad_qkv = jnp.concatenate(
        [from_groups(grad_query_groups, row_count, col_count), grad_pair_own], axis=-1
    ).astype(jnp.bfloat16)
    grad_qkv_weight = jnp.einsum(
        "brwd,brwe->de", conv_out, grad_qkv, preferred_element_type=jnp.float32
    )
    grad_conv_out = jnp.einsum(
        "brwe,de->brwd", grad_qkv, qkv_weight, preferred_element_type=jnp.float32
    ).astype(jnp.bfloat16)
    grad_conv_out_pad = with_halo(grad_conv_out, (("narrow", 1),), 1)
    grad_conv_attn, grad_hidden_in = depth_conv_grads(padded_in, grad_conv_out_pad, conv_attn)
    unused_one, norm_back_one = jax.vjp(modulate_norm, values_in, shift_one, scale_one)
    grad_from_one, grad_shift_one, grad_scale_one = norm_back_one(grad_hidden_in)
    grad_tokens = grad_mid + grad_from_one
    grad_modulation = jnp.concatenate(
        [
            grad_shift_one.reshape(image_count, channels),
            grad_scale_one.reshape(image_count, channels),
            grad_gate_one,
            grad_shift_two.reshape(image_count, channels),
            grad_scale_two.reshape(image_count, channels),
            grad_gate_two,
        ],
        axis=1,
    )
    grad_ada_weight = jnp.dot(cond_all.astype(jnp.float32).T, grad_modulation, precision=HIGH)
    grad_ada_bias = jnp.sum(grad_modulation, axis=0)
    totals = lax.psum(
        (
            grad_ada_weight,
            grad_ada_bias,
            grad_conv_attn,
            grad_qkv_weight,
            grad_proj_weight,
            grad_fc1_weight,
            grad_fc1_bias,
            grad_conv_ffn,
            grad_fc2_weight,
            grad_fc2_bias,
            grad_down_weight,
            grad_down_bias,
        ),
        ("wide", "narrow"),
    )
    return (
        result,
        grad_tokens,
        totals[0],
        totals[1],
        totals[2],
        totals[3],
        totals[4],
        totals[5],
        totals[6],
        totals[7],
        totals[8],
        totals[9],
        totals[10],
        totals[11],
    )


def solution(mesh):
    in_specs = (
        P("wide", "narrow", None, None),
        P("wide"),
        P(("wide", "narrow"), None, None, None),
        P(),
        P(),
        P(),
        P(),
        P(),
        P(),
        P(),
        P(),
        P(),
        P(),
        P(),
        P(),
    )
    out_specs = (
        P(("wide", "narrow"), None, None, None),
        P("wide", "narrow", None, None),
        P(),
        P(),
        P(),
        P(),
        P(),
        P(),
        P(),
        P(),
        P(),
        P(),
        P(),
        P(),
    )
    return jax.shard_map(shards, mesh=mesh, in_specs=in_specs, out_specs=out_specs, check_vma=False)
```

profile of v0, /device:TPU:0, one launch (start us, length us, event | category | flops | bytes accessed | tf_op | source)
XLA Modules:
  0.0 1774.4 jit_solution(31865291041044090)
XLA Ops:
  29.1 8.2 fusion.51
  39.1 5.6 convolution_convert_fusion
  54.6 7.2 all-to-all-start.1
  62.0 4.4 slice.345
  66.4 10.9 reshape.293
  77.3 8.4 copy.84
  85.8 133.5 %all-gather.2.cloned.1.call-done = bf16[16,32,32,768]{3,2,1,0:T(8,128)(2,1)} async-done(((bf16[16,8,32,768]{3,2,1,0:T(8,128)(2,1)}), bf16[16,32,32,768]{3,2,1,0:T(8,128)(2,1)}) %all-gather.2.cloned.1.call-update) | async-done | bytes 25165840 | tf_op jit(solution)/shard_map/all_gather | solution.py:164
  219.3 19.0 %fusion.96 = (bf16[16,32,32,384]{3,2,1,0:T(8,128)(2,1)}, bf16[16,32,32,384]{3,2,1,0:T(8,128)(2,1)}) fusion(bf16[16,32,32,768]{3,2,1,0:T(8,128)(2,1)} %all-gather.2.cloned.1.call-done), kind=kLoop, calls=%fused_computation.245 | loop fusion | bytes 50331648 | tf_op jit(solution)/shard_map/slice | solution.py:167
  238.2 38.1 %reshape.295 = bf16[16,16,2,16,2,6,64]{6,5,4,3,2,1,0:T(8,128)(2,1)} reshape(bf16[16,32,32,384]{3,2,1,0:T(8,128)(2,1)} %get-tuple-element.82) | data formatting | bytes 25165824 | tf_op jit(solution)/shard_map/reshape | solution.py:88
  276.4 19.8 %copy.85 = bf16[16,2,2,6,16,16,64]{6,5,4,3,2,1,0:T(8,128)(2,1)} copy(bf16[16,2,2,6,16,16,64]{6,3,2,5,1,4,0:T(8,128)(2,1)} %bitcast.172) | data formatting | bytes 25165824 | tf_op jit(solution)/shard_map/transpose | solution.py:89
  296.2 27.0 %multiply_reduce_fusion.1 = (f32[16,4,6,64]{3,2,1,0:T(8,128)S(1)}, f32[16,4,6,64,256]{4,3,2,1,0:T(8,128)}) fusion(bf16[16,4,6,64,64]{4,3,2,1,0:T(8,128)(2,1)} %bitcast.180, bf16[16,4,6,256,64]{4,3,2,1,0:T(8,128)(2,1)} %bitcast.170), kind=kOutput, calls=%fused_computation.63 | convolution fusion | flops 817864704 | bytes 40992768 | tf_op jit(solution)/shard_map/bghqe,bghke->bghqk/dot_general | solution.py:122
  323.2 12.0 exponential_reduce_fusion
  335.3 38.2 %reshape.297 = bf16[16,16,2,16,2,6,64]{6,5,4,3,2,1,0:T(8,128)(2,1)} reshape(bf16[16,32,32,384]{3,2,1,0:T(8,128)(2,1)} %get-tuple-element.83) | data formatting | bytes 25165824 | tf_op jit(solution)/shard_map/reshape | solution.py:88
  373.5 19.8 %copy.87 = bf16[16,2,2,6,16,16,64]{6,5,4,3,2,1,0:T(8,128)(2,1)} copy(bf16[16,2,2,6,16,16,64]{6,3,2,5,1,4,0:T(8,128)(2,1)} %bitcast.173) | data formatting | bytes 25165824 | tf_op jit(solution)/shard_map/transpose | solution.py:89
  393.4 22.2 %convolution_convert_fusion.2 = bf16[16,4,6,64,64]{4,3,2,1,0:T(8,128)(2,1)} fusion(bf16[16,4,6,256,64]{4,3,2,1,0:T(8,128)(2,1)} %bitcast.168, f32[16,4,6,64,256]{4,3,2,1,0:T(8,128)} %get-tuple-element.105, f32[16,4,6,64]{3,2,1,0:T(8,128)S(1)} %log_add_fusion), kind=kOutput, calls=%fused_computation.160 | convolution fusion | flops 825753600 | bytes 40992768 | tf_op jit(solution)/shard_map/bghqk,bghke->bghqe/dot_general | solution.py:173
  415.6 15.2 copy.132
  430.8 11.6 convert_element_type.482
  442.4 8.2 fusion.95
  453.4 8.9 add_convert_fusion
  462.3 4.6 copy-done.5
  475.3 5.6 convert_reduce_fusion.2
  480.9 8.9 copy.94
  489.8 8.5 reshape.299
  498.3 15.1 select_maximum_fusion.2
  513.4 52.4 %fusion.8 = f32[16,8,32,1536]{3,2,1,0:T(8,128)} fusion(bf16[16,8,32,1536]{3,2,1,0:T(8,128)(2,1)} %copy-done.5, bf16[16,1,32,1536]{3,2,1,0:T(8,128)(2,1)} %collective-permute-done.3, bf16[16,1,32,1536]{3,2,1,0:T(8,128)(2,1)} %collective-permute-done.2, f32[1536]{0:T(1024)S(1)} %get-tuple-element.51, f32[1536]{0:T(1024)S(1)} %get-tuple-element.52, ...), kind=kLoop, calls=%fused_computation.31 | loop fusion | flops 176160768 | bytes 116447232 | tf_op jit(solution)/shard_map/add | solution.py:58
  565.8 64.6 %fusion.22 = (f32[1536]{0:T(1024)}, f32[1536]{0:T(1024)}, f32[1536]{0:T(1024)}, f32[1536]{0:T(1024)}, f32[1536]{0:T(1024)}, /*index=5*/f32[1536]{0:T(1024)}, f32...) fusion(bf16[16,10,34,1536]{3,2,1,0:T(8,128)(2,1)} %select_maximum_fusion.2, ...), kind=kOutput, calls=%fused_computation.45 | convolution fusion | flops 5149542912 | bytes 136525824 | tf_op jit(solution)/shard_map/brwd,fd->brwf/dot_general | solution.py:211
  641.0 20.7 %select_maximum_fusion = bf16[16,10,34,1536]{3,2,1,0:T(8,128)(2,1)} fusion(bf16[16,1,32,1536]{3,2,1,0:T(8,128)(2,1)S(1)} %collective-permute-done.5, bf16[16,8,32,1536]{3,2,1,0:T(8,128)(2,1)} %get-tuple-element.112, bf16[16,1,32,1536]{3,2,1,0:T(8,128)(2,1)S(1)} %collective-permute-done.4), kind=kLoop, calls=%fused_computation.74 | loop fusion | flops 100270080 | bytes 32440320 | tf_op jit(solution)/shard_map/concatenate | solution.py:21
  661.7 50.8 %convert_reduce_fusion = (f32[1536]{0:T(1024)}, bf16[16,8,32,1536]{3,2,1,0:T(8,128)(2,1)}) fusion(f32[1536]{0:T(1024)S(1)} %get-tuple-element.51, bf16[16,10,34,1536]{3,2,1,0:T(8,128)(2,1)} %select_maximum_fusion, f32[1536]{0:T(1024)S(1)} %get-tuple-element.52, bf16[16,8,32,1536]{3,2,1,0:T(8,128)(2,1)} %get-tuple-element.112, ...), kind=kLoop, calls=%fused_computation.55 | loop fusion | flops 195033600 | bytes 103870464 | tf_op jit(solution)/shard_map/reduce_sum | solution.py:222
  712.5 11.4 multiply_reduce_fusion.5
  723.9 6.3 multiply_reduce_fusion.3
  730.3 19.9 %multiply_reduce_fusion.2 = (f32[16,384]{1,0:T(8,128)}, bf16[16,8,32,384]{3,2,1,0:T(8,128)(2,1)}, f32[16,384]{1,0:T(8,128)}, f32[16,8,32,384]{3,2,1,0:T(8,128)S(1)}) fusion(f32[16,8,32,384]{3,2,1,0:T(8,128)} %reshape.299, f32[384]{0:T(512)S(1)} %convert_element_type.514, f32[16,8,32,384]{3,2,1,0:T(8,128)} %copy-done.6, f32[16,384]{1,0:T(8,128)S(1)} %copy-done.61, ...), kind=kOutput, calls=%fused_computation.143 | convolution fusion | flops 4913614848 | bytes 61113856 | tf_op jit(solution)/shard_map/dot_general | solution.py:187
  756.7 10.6 reshape.300
  767.3 7.8 copy.95
  775.0 28.2 %multiply_reduce_fusion = (f32[16,4,6,64]{3,2,1,0:T(8,128)S(1)}, f32[16,4,6,64,256]{4,3,2,1,0:T(8,128)}) fusion(f32[16,4,6,64,256]{4,3,2,1,0:T(8,128)} %get-tuple-element.105, f32[16,4,6,64]{3,2,1,0:T(8,128)S(1)} %copy-done.15, bf16[16,4,6,64,64]{4,3,2,1,0:T(8,128)(2,1)} %bitcast.178, bf16[16,4,6,256,64]{4,3,2,1,0:T(8,128)(2,1)} %bitcast.169), kind=kOutput, calls=%fused_computation.58 | convolution fusion | flops 830447616 | bytes 66256896 | tf_op jit(solution)/shard_map/bghqe,bghke->bghqk/dot_general | solution.py:241
  803.2 18.2 %convolution_convert_fusion.1 = bf16[16,4,6,256,64]{3,4,2,1,0:T(8,128)(2,1)} fusion(bf16[16,4,6,64,64]{4,3,2,1,0:T(8,128)(2,1)} %bitcast.179, f32[16,4,6,64,256]{4,3,2,1,0:T(8,128)} %get-tuple-element.105, f32[16,4,6,64]{3,2,1,0:T(8,128)S(1)} %copy-done.15), kind=kOutput, calls=%fused_computation.111 | convolution fusion | flops 830472192 | bytes 40992768 | tf_op jit(solution)/shard_map/bghqk,bghqe->bghke/dot_general | solution.py:244
  821.4 21.7 %multiply_convert_fusion.1 = bf16[16,4,6,64,256]{4,3,2,1,0:T(8,128)(2,1)} fusion(f32[16,4,6,64,256]{4,3,2,1,0:T(8,128)} %get-tuple-element.110, f32[16,4,6,64,256]{4,3,2,1,0:T(8,128)} %get-tuple-element.105, f32[16,4,6,64]{3,2,1,0:T(8,128)S(1)} %get-tuple-element.109, f32[16,4,6,64]{3,2,1,0:T(8,128)S(1)} %copy-done.15), kind=kLoop, calls=%fused_computation.57 | loop fusion | flops 31457280 | bytes 63111168 | tf_op jit(solution)/shard_map/convert_element_type | solution.py:248
  843.1 10.9 multiply_convert_fusion
  854.0 22.9 %copy.100 = bf16[16,4,6,256,64]{4,3,2,1,0:T(8,128)(2,1)} copy(bf16[16,4,6,256,64]{3,4,2,1,0:T(8,128)(2,1)} %multiply_convert_fusion) | data formatting | bytes 25165824 | tf_op jit(solution)/shard_map/convert.30
  876.9 36.9 %copy.101 = bf16[16,16,2,16,2,6,64]{6,5,4,3,2,1,0:T(8,128)(2,1)} copy(bf16[16,16,2,16,2,6,64]{6,3,1,5,4,2,0:T(8,128)(2,1)} %bitcast.175) | data formatting | bytes 25165824 | tf_op jit(solution)/shard_map/transpose | solution.py:98
  913.8 40.4 %reshape.305 = bf16[16,32,32,384]{3,2,1,0:T(8,128)(2,1)} reshape(bf16[16,16,2,16,2,6,64]{6,5,4,3,2,1,0:T(8,128)(2,1)} %copy.101) | data formatting | bytes 25165824 | tf_op jit(solution)/shard_map/reshape | solution.py:99
  954.3 22.9 %copy.103 = bf16[16,4,6,256,64]{4,3,2,1,0:T(8,128)(2,1)} copy(bf16[16,4,6,256,64]{3,4,2,1,0:T(8,128)(2,1)} %convolution_convert_fusion.1) | data formatting | bytes 25165824 | tf_op jit(solution)/shard_map/convert.27
  977.2 36.9 %copy.104 = bf16[16,16,2,16,2,6,64]{6,5,4,3,2,1,0:T(8,128)(2,1)} copy(bf16[16,16,2,16,2,6,64]{6,3,1,5,4,2,0:T(8,128)(2,1)} %bitcast.176) | data formatting | bytes 25165824 | tf_op jit(solution)/shard_map/transpose | solution.py:98
  1014.1 40.9 %reshape.307 = bf16[16,32,32,384]{3,2,1,0:T(8,128)(2,1)} reshape(bf16[16,16,2,16,2,6,64]{6,5,4,3,2,1,0:T(8,128)(2,1)} %copy.104) | data formatting | bytes 25165824 | tf_op jit(solution)/shard_map/reshape | solution.py:99
  1054.9 20.9 %pad_maximum_fusion = bf16[16,32,32,768]{3,2,1,0:T(8,128)(2,1)} fusion(bf16[16,32,32,384]{3,2,1,0:T(8,128)(2,1)} %reshape.307, bf16[16,32,32,384]{3,2,1,0:T(8,128)(2,1)} %reshape.305), kind=kLoop, calls=%fused_computation.54 | loop fusion | flops 50331648 | bytes 50331648 | tf_op jit(solution)/shard_map/concatenate | solution.py:256
  1075.8 12.5 copy.123
  1088.3 15.7 copy.125
  1107.3 17.7 convolution_bitcast_fusion.1
  1125.0 7.4 convert_element_type.516
  1132.4 7.3 copy.90
  1139.7 8.3 convert_element_type.518
  1148.0 20.3 %multiply_convert_fusion.3 = bf16[16,4,6,64,64]{4,3,2,1,0:T(8,128)(2,1)} fusion(bf16[16,4,6,64,256]{4,3,2,1,0:T(8,128)(2,1)} %multiply_convert_fusion.1, bf16[16,4,6,256,64]{4,3,2,1,0:T(8,128)(2,1)} %bitcast.171), kind=kOutput, calls=%fused_computation.87 | convolution fusion | flops 808452096 | bytes 28311552 | tf_op jit(solution)/shard_map/bghqk,bghke->bghqe/dot_general | solution.py:250
  1168.3 15.2 copy.131
  1183.5 11.4 reshape.303
  1199.0 6.9 convolution_bitcast_fusion.5
  1205.9 4.4 convolution_bitcast_fusion
  1212.2 7.0 convolution_bitcast_fusion.2
  1219.2 82.2 %reduce-scatter.5.cloned.1.call-done = bf16[8,393216]{1,0:T(8,128)(2,1)} async-done(((bf16[32,393216]{1,0:T(8,128)(2,1)}), bf16[8,393216]{1,0:T(8,128)(2,1)}) %reduce-scatter.5.cloned.1.call-update) | async-done | bytes 6291472
  1309.1 21.1 %fusion.59 = (f32[384]{0:T(512)S(1)}, f32[384]{0:T(512)S(1)}, f32[384]{0:T(512)S(1)}, f32[384]{0:T(512)S(1)}, f32[384]{0:T(512)S(1)}, /*index=5*/f32[384]{0:T(51...) fusion(bf16[16,10,34,384]{3,2,1,0:T(8,128)(2,1)} %copy-done.4, ...), kind=kOutput, calls=%fused_computation.131 | convolution fusion | flops 3672632832 | bytes 36288000 | tf_op jit(solution)/shard_map/brwe,de->brwd/dot_general | solution.py:272
  1334.7 10.1 convolution_bitcast_fusion.3
  1348.6 9.5 fusion.53
  1366.0 4.6 add_convert_fusion.3
  1370.7 24.3 %all_to_all.36 = bf16[16,4,16,768]{3,2,1,0:T(8,128)(2,1)S(1)} all-to-all(bf16[16,4,16,768]{3,2,1,0:T(8,128)(2,1)S(1)} %add_convert_fusion.3), channel_id=1, replica_groups=mesh['wide'=8,'narrow'=4] {'narrow'}, dimensions={0} | all-to-all | bytes 3145728 | tf_op jit(solution)/shard_map/all_to_all | solution.py:196
  1400.7 89.1 %all-reduce.9.cloned.1.call-done = (f32[2304]{0:T(1024)}, f32[3,3,384]{2,1,0:T(4,128)}, f32[1536]{0:T(1024)}, f32[3,3,1536]{2,1,0:T(4,128)}, f32[384]{0:T(512)}, /*index=5*/f32[768]{0:T(1024)}) async-done(((f32[2304]{0:T(1024)}, f32[3,3,384]{2,1,0:T(4,128)}, f32[1536]{0:T(1024)}, f32[3,3,1536]{2,1,0:T(4,128)}, f32[384]{0:T(512)}, /*index=5*/f32[768]{0:T(1024)}), (f32[2304]{0:T(1024)}, ...) | async-done | bytes 89104 | tf_op jit(solution)/shard_map/psum | solution.py:293
  1489.8 260.7 %all-reduce.11.cloned.1.call-done = (f32[256,2304]{1,0:T(8,128)}, f32[384,1152]{1,0:T(8,128)}, f32[384,384]{1,0:T(8,128)}, f32[384,1536]{1,0:T(8,128)}, f32[1536,384]{1,0:T(8,128)}, /*index=5*/f32[1536,768]{1,0:T(8,128)}) async-done(((f32[256,2304]{1,0:T(8,128)}, f32[384,1152]{1,0:T(8,128)}, f32[384,384]{1,0:T(8,128)}, f32[384,1536]{1,0:T(8,128)}, f32[1536,384]{1,0:T(8,128)}, ...) | async-done | bytes 14155792 | tf_op jit(solution)/shard_map/psum | solution.py:293
  (342 shorter events, 116.7 us)
Async XLA Ops:
  7.2 468.1 %copy-start = (bf16[1536,768]{1,0:T(8,128)(2,1)S(1)}, bf16[1536,768]{1,0:T(8,128)(2,1)}, u32[]{:S(2)}) copy-start(bf16[1536,768]{1,0:T(8,128)(2,1)} %param.28) | copy-start | bytes 7077892
  7.2 212.1 %all-gather.2.cloned.1.call-start = ((), (), s32[]{:S(2)}) async-start(), calls=%async_computation.3 | async-start | bytes 31457280 | tf_op jit(solution)/shard_map/all_gather | solution.py:164
  7.2 9.1 copy-start.1
  11.9 10.2 copy-start.65
  14.8 14.2 copy-start.30
  15.0 14.1 copy-start.54
  15.0 14.1 copy-start.56
  16.3 12.7 copy-start.32
  18.2 19.0 %copy-start.8 = (bf16[16,8,32,384]{3,2,1,0:T(8,128)(2,1)}, bf16[16,8,32,384]{3,2,1,0:T(8,128)(2,1)S(1)}, u32[]{:S(2)}) copy-start(bf16[16,8,32,384]{3,2,1,0:T(8,128)(2,1)S(1)} %fusion.41) | copy-start | bytes 9437188
  18.4 3.8 collective-permute-start
  20.8 5.7 collective-permute-start.1
  22.1 15.2 copy-start.66
  22.1 15.2 copy-start.68
  22.1 15.2 copy-start.70
  22.1 15.2 copy-start.72
  22.2 15.2 copy-start.74
  22.2 15.2 copy-start.76
  22.2 15.2 copy-start.78
  22.2 15.2 copy-start.80
  22.2 15.2 copy-start.82
  22.2 15.1 copy-start.21
  26.5 10.9 copy-start.23
  29.1 10.0 copy-start.102
  51.8 10.2 copy-start.94
  54.6 419.1 %all-to-all-start.1 = ((bf16[4,16,16,768]{3,2,0,1:T(8,128)(2,1)}), bf16[4,16,16,768]{3,2,0,1:T(8,128)(2,1)}, u32[]{:S(2)}, u32[]{:S(2)}) async-start(bf16[4,16,16,768]{3,2,0,1:T(8,128)(2,1)} %copy.92), calls=%async_computation.1 | async-start | bytes 3145728 | tf_op jit(solution)/shard_map/all_to_all | solution.py:197
  61.8 1239.6 %reduce-scatter.5.cloned.1.call-start = ((), (), s32[]{:S(2)}) async-start(), calls=%async_computation.4 | async-start | bytes 31457280
  335.3 58.1 %copy-start.14 = (f32[16,4,6,64]{3,2,1,0:T(8,128)}, f32[16,4,6,64]{3,2,1,0:T(8,128)S(1)}, u32[]{:S(2)}) copy-start(f32[16,4,6,64]{3,2,1,0:T(8,128)S(1)} %log_add_fusion) | copy-start | bytes 294916
  430.8 11.6 copy-start.28
  430.8 11.6 copy-start.45
  450.7 11.6 copy-start.34
  452.1 10.2 copy-start.42
  466.9 8.4 copy-start.61
  468.9 29.4 %collective-permute-start.2 = (bf16[16,1,32,1536]{3,2,1,0:T(8,128)(2,1)}, bf16[16,1,32,1536]{3,2,1,0:T(8,128)(2,1)}, u32[]{:S(2)}, u32[]{:S(2)}) collective-permute-start(bf16[16,1,32,1536]{3,2,1,0:T(8,128)(2,1)} %get-tuple-element.86), channel_id=1, source_target_pairs={{0,1},{1,2},{2,3},{4,5},{5,6},{6,7},{8,9},{9,10},{10,11},{12,13},{... | collective-permute-start | bytes 4718600 | tf_op jit(solution)/shard_map/ppermute | solution.py:17
  472.2 26.1 %collective-permute-start.3 = (bf16[16,1,32,1536]{3,2,1,0:T(8,128)(2,1)}, bf16[16,1,32,1536]{3,2,1,0:T(8,128)(2,1)}, u32[]{:S(2)}, u32[]{:S(2)}) collective-permute-start(bf16[16,1,32,1536]{3,2,1,0:T(8,128)(2,1)} %get-tuple-element.87), channel_id=1, source_target_pairs={{1,0},{2,1},{3,2},{5,4},{6,5},{7,6},{9,8},{10,9},{11,10},{13,12},{... | collective-permute-start | bytes 4718600 | tf_op jit(solution)/shard_map/ppermute | solution.py:20
  513.4 52.4 %copy-start.100 = (bf16[1536,384]{1,0:T(8,128)(2,1)S(1)}, bf16[1536,384]{1,0:T(8,128)(2,1)}, u32[]{:S(2)}) copy-start(bf16[1536,384]{1,0:T(8,128)(2,1)} %param.26) | copy-start | bytes 3538948
  632.6 6.0 collective-permute-start.4
  635.7 5.3 collective-permute-start.5
  661.7 50.8 %copy-start.35 = (f32[16,8,32]{2,1,0:T(8,128)S(1)}, f32[16,8,32]{2,1,0:T(8,128)}, u32[]{:S(2)}) copy-start(f32[16,8,32]{2,1,0:T(8,128)} %copy-done.34) | copy-start | bytes 49156
  661.7 50.8 %copy-start.49 = (f32[16,384]{1,0:T(8,128)S(1)}, f32[16,384]{1,0:T(8,128)}, u32[]{:S(2)}) copy-start(f32[16,384]{1,0:T(8,128)} %get-tuple-element.98) | copy-start | bytes 73732
  712.5 11.4 copy-start.38
  712.5 11.4 copy-start.43
  730.2 22.7 %copy-start.29 = (bf16[384,384]{1,0:T(8,128)(2,1)S(1)}, bf16[384,384]{1,0:T(8,128)(2,1)}, u32[]{:S(2)}) copy-start(bf16[384,384]{1,0:T(8,128)(2,1)} %param.22) | copy-start | bytes 884740
  730.2 22.7 %copy-start.46 = (f32[16,384]{1,0:T(8,128)S(1)}, f32[16,384]{1,0:T(8,128)}, u32[]{:S(2)}) copy-start(f32[16,384]{1,0:T(8,128)} %get-tuple-element.101) | copy-start | bytes 73732
  1104.1 385.7 %all-reduce.9.cloned.1.call-start = ((), (), s32[]{:S(2)}) async-start(), calls=%async_computation.5 | async-start | bytes 237568 | tf_op jit(solution)/shard_map/psum | solution.py:293
  1183.5 15.4 copy-start.47
  1198.9 11.4 slice-start
  1199.0 11.4 slice-start.6
  1331.4 14.4 collective-permute-start.6
  1333.2 12.6 copy-start.12
  1333.2 12.6 collective-permute-start.7
  1348.6 9.6 copy-start.40
  1348.6 9.6 copy-start.31
  1362.7 387.7 %all-reduce.11.cloned.1.call-start = ((), (), s32[]{:S(2)}) async-start(), calls=%async_computation.6 | async-start | bytes 28311552 | tf_op jit(solution)/shard_map/psum | solution.py:293
  1366.0 30.3 %slice-start.2 = ((s8[6291456]{0:T(1024)(128)(4,1)}), s8[4194304]{0:T(1024)(128)(4,1)S(1)}, s32[]{:S(2)}) async-start(s8[6291456]{0:T(1024)(128)(4,1)} %bitcast.184), calls=%async_computation.9 | async-start | bytes 8388608
  1366.0 30.3 %slice-start.4 = ((s8[6291456]{0:T(1024)(128)(4,1)}), s8[4194304]{0:T(1024)(128)(4,1)S(1)}, s32[]{:S(2)}) async-start(s8[6291456]{0:T(1024)(128)(4,1)} %bitcast.193), calls=%async_computation.11 | async-start | bytes 8388608
  1366.0 30.3 %slice-start.3 = ((s8[6291456]{0:T(1024)(128)(4,1)}), s8[2097152]{0:T(1024)(128)(4,1)S(1)}, s32[]{:S(2)}) async-start(s8[6291456]{0:T(1024)(128)(4,1)} %bitcast.184), calls=%async_computation.10 | async-start | bytes 4194304
  1366.0 30.3 %slice-start.5 = ((s8[6291456]{0:T(1024)(128)(4,1)}), s8[2097152]{0:T(1024)(128)(4,1)S(1)}, s32[]{:S(2)}) async-start(s8[6291456]{0:T(1024)(128)(4,1)} %bitcast.193), calls=%async_computation.12 | async-start | bytes 4194304
  1370.7 25.6 %copy-start.3 = (bf16[16,8,32,384]{3,2,1,0:T(8,128)(2,1)S(1)}, bf16[16,8,32,384]{3,2,1,0:T(8,128)(2,1)}, u32[]{:S(2)}) copy-start(bf16[16,8,32,384]{3,2,1,0:T(8,128)(2,1)} %param.15) | copy-start | bytes 9437188
  1750.4 9.0 copy-start.41
  1750.4 9.8 copy-start.20
  1750.4 11.2 copy-start.93
  1750.4 11.8 copy-start.58
  1750.4 12.4 copy-start.19
  1756.5 8.4 slice-start.9
  (63 other events, 260.9 us)
Sparse Core Ops, SparseCore 0:
  52.0 167.2 all-gather.1
  1104.2 197.1 reduce-scatter.4
  1362.8 126.8 all-reduce.8
  1498.3 252.0 all-reduce.10
where the time goes:
time: 1790 us; the launch traced here: 1770 us
  waiting for transfers between devices  574 us (32%)
  local copies, waits for them, and re-layouts  561 us (31%)
  matrix products  329 us (18%)
  other arithmetic  247 us (14%)
  blocking collectives  24.3 us (1%)
  starting transfers between devices  23.5 us (1%)
    psum x2, waiting for transfers between devices, shards(): lax.psum((grad_ada_weight, grad_ada_bias, grad_conv_attn, grad_qkv_weight...  350 us
    all_gather x1, waiting for transfers between devices, shards(): pair_all = lax.all_gather(pair_own, 'narrow', axis=1, tiled=True)  133 us
    reshape x4, local copies, waits for them, and re-layouts, to_groups(): values.reshape(batch_size, row_count // 2, 2, col_count // 2, 2, head_cou...  97.9 us
    reshape x3, local copies, waits for them, and re-layouts, from_groups(): shaped.reshape(batch_size, row_count, col_count, head_count * head_size)  92.7 us
    unnamed x5, waiting for transfers between devices  82.3 us
    transpose x2, local copies, waits for them, and re-layouts, from_groups(): shaped = shaped.transpose(0, 4, 1, 5, 2, 3, 6)  73.8 us
    unnamed x250, local copies, waits for them, and re-layouts  73.6 us
    dot_general x1, matrix products, shards(): jnp.einsum('brwd,fd->brwf', grad_ffn_out, fc2_weight, preferred_element_t...  64.6 us
  transfers between devices with their start and end apart: 13, of which 7 were waited for; matrix products, arithmetic and copies ran while one was open for 24% of the time, Pallas kernels for 0%

commit v1 on v0

--- a/solution.py
+++ b/solution.py
@@ -290,23 +290,22 @@
     )
     grad_ada_weight = jnp.dot(cond_all.astype(jnp.float32).T, grad_modulation, precision=HIGH)
     grad_ada_bias = jnp.sum(grad_modulation, axis=0)
-    totals = lax.psum(
-        (
-            grad_ada_weight,
-            grad_ada_bias,
-            grad_conv_attn,
-            grad_qkv_weight,
-            grad_proj_weight,
-            grad_fc1_weight,
-            grad_fc1_bias,
-            grad_conv_ffn,
-            grad_fc2_weight,
-            grad_fc2_bias,
-            grad_down_weight,
-            grad_down_bias,
-        ),
-        ("wide", "narrow"),
-    )
+    totals = (
+        grad_ada_weight,
+        grad_ada_bias,
+        grad_conv_attn,
+        grad_qkv_weight,
+        grad_proj_weight,
+        grad_fc1_weight,
+        grad_fc1_bias,
+        grad_conv_ffn,
+        grad_fc2_weight,
+        grad_fc2_bias,
+        grad_down_weight,
+        grad_down_bias,
+    )
+    for jj in ("narrow", "wide"):
+        totals = lax.psum(totals, jj)
     return (
         result,
         grad_tokens,

time: 1790 us -> 2210 us (1.23)
  waiting for transfers between devices: 574 us -> 997 us
    psum x2 -> x4, waiting for transfers between devices: 350 us -> 773 us  [shards(): totals = lax.psum(totals, jj)]
    unnamed x5 -> x7, waiting for transfers between devices: 82.3 us -> 82.3 us
  transfers between devices with their start and end apart: 13 -> 15, of which waited for: 7 -> 9; matrix products, arithmetic and copies ran while one was open for 24% -> 20% of each run, Pallas kernels for 0% -> 0%
where the time goes in v1:
time: 2210 us; the launch traced here: 2200 us
  waiting for transfers between devices  997 us (45%)
  local copies, waits for them, and re-layouts  561 us (25%)
  matrix products  329 us (15%)
  other arithmetic  247 us (11%)
  starting transfers between devices  23.6 us (1%)
  blocking collectives  22.8 us (1%)
    psum x4, waiting for transfers between devices, shards(): totals = lax.psum(totals, jj)  773 us
    all_gather x1, waiting for transfers between devices, shards(): pair_all = lax.all_gather(pair_own, 'narrow', axis=1, tiled=True)  133 us
    reshape x4, local copies, waits for them, and re-layouts, to_groups(): values.reshape(batch_size, row_count // 2, 2, col_count // 2, 2, head_cou...  97.9 us
    reshape x3, local copies, waits for them, and re-layouts, from_groups(): shaped.reshape(batch_size, row_count, col_count, head_count * head_size)  92.7 us
    unnamed x7, waiting for transfers between devices  82.3 us
    transpose x2, local copies, waits for them, and re-layouts, from_groups(): shaped = shaped.transpose(0, 4, 1, 5, 2, 3, 6)  73.8 us
    unnamed x250, local copies, waits for them, and re-layouts  73.6 us
    dot_general x1, matrix products, shards(): jnp.einsum('brwd,fd->brwf', grad_ffn_out, fc2_weight, preferred_element_t...  64.6 us
  transfers between devices with their start and end apart: 15, of which 9 were waited for; matrix products, arithmetic and copies ran while one was open for 20% of the time, Pallas kernels for 0%

profile of v1, /device:TPU:0, one launch (start us, length us, event | category | flops | bytes accessed | tf_op | source)
XLA Modules:
  0.0 2196.9 jit_solution(17467162345358427233)
XLA Ops:
  29.1 8.2 fusion.51
  39.1 5.6 convolution_convert_fusion
  54.6 7.2 all-to-all-start.1
  66.4 10.9 reshape.293
  77.3 8.4 copy.84
  85.8 133.5 %all-gather.2.cloned.1.call-done = bf16[16,32,32,768]{3,2,1,0:T(8,128)(2,1)} async-done(((bf16[16,8,32,768]{3,2,1,0:T(8,128)(2,1)}), bf16[16,32,32,768]{3,2,1,0:T(8,128)(2,1)}) %all-gather.2.cloned.1.call-update) | async-done | bytes 25165840 | tf_op jit(solution)/shard_map/all_gather | solution.py:164
  219.3 19.0 fusion.96
  238.2 38.1 %reshape.295 = bf16[16,16,2,16,2,6,64]{6,5,4,3,2,1,0:T(8,128)(2,1)} reshape(bf16[16,32,32,384]{3,2,1,0:T(8,128)(2,1)} %get-tuple-element.94) | data formatting | bytes 25165824 | tf_op jit(solution)/shard_map/reshape | solution.py:88
  276.4 19.8 copy.85
  296.2 27.0 %multiply_reduce_fusion.1 = (f32[16,4,6,64]{3,2,1,0:T(8,128)S(1)}, f32[16,4,6,64,256]{4,3,2,1,0:T(8,128)}) fusion(bf16[16,4,6,64,64]{4,3,2,1,0:T(8,128)(2,1)} %bitcast.180, bf16[16,4,6,256,64]{4,3,2,1,0:T(8,128)(2,1)} %bitcast.170), kind=kOutput, calls=%fused_computation.63 | convolution fusion | flops 817864704 | bytes 40992768 | tf_op jit(solution)/shard_map/bghqe,bghke->bghqk/dot_general | solution.py:122
  323.2 12.0 exponential_reduce_fusion
  335.3 38.2 %reshape.297 = bf16[16,16,2,16,2,6,64]{6,5,4,3,2,1,0:T(8,128)(2,1)} reshape(bf16[16,32,32,384]{3,2,1,0:T(8,128)(2,1)} %get-tuple-element.95) | data formatting | bytes 25165824 | tf_op jit(solution)/shard_map/reshape | solution.py:88
  373.5 19.8 copy.87
  393.4 22.2 %convolution_convert_fusion.2 = bf16[16,4,6,64,64]{4,3,2,1,0:T(8,128)(2,1)} fusion(bf16[16,4,6,256,64]{4,3,2,1,0:T(8,128)(2,1)} %bitcast.168, f32[16,4,6,64,256]{4,3,2,1,0:T(8,128)} %get-tuple-element.117, f32[16,4,6,64]{3,2,1,0:T(8,128)S(1)} %log_add_fusion), kind=kOutput, calls=%fused_computation.160 | convolution fusion | flops 825753600 | bytes 40992768 | tf_op jit(solution)/shard_map/bghqk,bghke->bghqe/dot_general | solution.py:173
  415.6 15.2 copy.132
  430.8 11.6 convert_element_type.482
  442.4 8.2 fusion.95
  453.4 8.9 add_convert_fusion
  462.3 4.6 copy-done.5
  475.3 5.6 convert_reduce_fusion.2
  480.9 8.9 copy.94
  489.8 8.5 reshape.299
  498.3 15.1 select_maximum_fusion.2
  513.4 52.4 %fusion.8 = f32[16,8,32,1536]{3,2,1,0:T(8,128)} fusion(bf16[16,8,32,1536]{3,2,1,0:T(8,128)(2,1)} %copy-done.5, bf16[16,1,32,1536]{3,2,1,0:T(8,128)(2,1)} %collective-permute-done.3, bf16[16,1,32,1536]{3,2,1,0:T(8,128)(2,1)} %collective-permute-done.2, f32[1536]{0:T(1024)S(1)} %get-tuple-element.51, f32[1536]{0:T(1024)S(1)} %get-tuple-element.52, ...), kind=kLoop, calls=%fused_computation.31 | loop fusion | flops 176160768 | bytes 116447232 | tf_op jit(solution)/shard_map/add | solution.py:58
  565.8 64.6 %fusion.22 = (f32[1536]{0:T(1024)}, f32[1536]{0:T(1024)}, f32[1536]{0:T(1024)}, f32[1536]{0:T(1024)}, f32[1536]{0:T(1024)}, /*index=5*/f32[1536]{0:T(1024)}, f32...) fusion(bf16[16,10,34,1536]{3,2,1,0:T(8,128)(2,1)} %select_maximum_fusion.2, ...), kind=kOutput, calls=%fused_computation.45 | convolution fusion | flops 5149542912 | bytes 136525824 | tf_op jit(solution)/shard_map/brwd,fd->brwf/dot_general | solution.py:211
  641.0 20.7 select_maximum_fusion
  661.7 50.8 %convert_reduce_fusion = (f32[1536]{0:T(1024)}, bf16[16,8,32,1536]{3,2,1,0:T(8,128)(2,1)}) fusion(f32[1536]{0:T(1024)S(1)} %get-tuple-element.51, bf16[16,10,34,1536]{3,2,1,0:T(8,128)(2,1)} %select_maximum_fusion, f32[1536]{0:T(1024)S(1)} %get-tuple-element.52, bf16[16,8,32,1536]{3,2,1,0:T(8,128)(2,1)} %get-tuple-element.124, ...), kind=kLoop, calls=%fused_computation.55 | loop fusion | flops 195033600 | bytes 103870464 | tf_op jit(solution)/shard_map/reduce_sum | solution.py:222
  712.5 11.4 multiply_reduce_fusion.5
  723.9 6.3 multiply_reduce_fusion.3
  730.3 19.9 multiply_reduce_fusion.2
  756.7 10.6 reshape.300
  767.3 7.8 copy.95
  775.0 28.2 %multiply_reduce_fusion = (f32[16,4,6,64]{3,2,1,0:T(8,128)S(1)}, f32[16,4,6,64,256]{4,3,2,1,0:T(8,128)}) fusion(f32[16,4,6,64,256]{4,3,2,1,0:T(8,128)} %get-tuple-element.117, f32[16,4,6,64]{3,2,1,0:T(8,128)S(1)} %copy-done.15, bf16[16,4,6,64,64]{4,3,2,1,0:T(8,128)(2,1)} %bitcast.178, bf16[16,4,6,256,64]{4,3,2,1,0:T(8,128)(2,1)} %bitcast.169), kind=kOutput, calls=%fused_computation.58 | convolution fusion | flops 830447616 | bytes 66256896 | tf_op jit(solution)/shard_map/bghqe,bghke->bghqk/dot_general | solution.py:241
  803.2 18.2 convolution_convert_fusion.1
  821.4 21.7 multiply_convert_fusion.1
  843.1 10.9 multiply_convert_fusion
  854.0 22.9 %copy.100 = bf16[16,4,6,256,64]{4,3,2,1,0:T(8,128)(2,1)} copy(bf16[16,4,6,256,64]{3,4,2,1,0:T(8,128)(2,1)} %multiply_convert_fusion) | data formatting | bytes 25165824 | tf_op jit(solution)/shard_map/convert.30
  876.9 36.9 %copy.101 = bf16[16,16,2,16,2,6,64]{6,5,4,3,2,1,0:T(8,128)(2,1)} copy(bf16[16,16,2,16,2,6,64]{6,3,1,5,4,2,0:T(8,128)(2,1)} %bitcast.175) | data formatting | bytes 25165824 | tf_op jit(solution)/shard_map/transpose | solution.py:98
  913.8 40.4 %reshape.305 = bf16[16,32,32,384]{3,2,1,0:T(8,128)(2,1)} reshape(bf16[16,16,2,16,2,6,64]{6,5,4,3,2,1,0:T(8,128)(2,1)} %copy.101) | data formatting | bytes 25165824 | tf_op jit(solution)/shard_map/reshape | solution.py:99
  954.3 22.9 %copy.103 = bf16[16,4,6,256,64]{4,3,2,1,0:T(8,128)(2,1)} copy(bf16[16,4,6,256,64]{3,4,2,1,0:T(8,128)(2,1)} %convolution_convert_fusion.1) | data formatting | bytes 25165824 | tf_op jit(solution)/shard_map/convert.27
  977.2 36.9 %copy.104 = bf16[16,16,2,16,2,6,64]{6,5,4,3,2,1,0:T(8,128)(2,1)} copy(bf16[16,16,2,16,2,6,64]{6,3,1,5,4,2,0:T(8,128)(2,1)} %bitcast.176) | data formatting | bytes 25165824 | tf_op jit(solution)/shard_map/transpose | solution.py:98
  1014.1 40.9 %reshape.307 = bf16[16,32,32,384]{3,2,1,0:T(8,128)(2,1)} reshape(bf16[16,16,2,16,2,6,64]{6,5,4,3,2,1,0:T(8,128)(2,1)} %copy.104) | data formatting | bytes 25165824 | tf_op jit(solution)/shard_map/reshape | solution.py:99
  1054.9 20.9 pad_maximum_fusion
  1075.8 12.5 copy.123
  1088.3 15.7 copy.125
  1107.3 17.7 convolution_bitcast_fusion.1
  1125.0 7.4 convert_element_type.516
  1132.4 7.3 copy.90
  1139.7 8.3 convert_element_type.518
  1148.0 20.3 multiply_convert_fusion.3
  1168.3 15.2 copy.131
  1183.5 11.4 reshape.303
  1199.0 6.9 convolution_bitcast_fusion.5
  1212.2 7.0 convolution_bitcast_fusion.2
  1219.2 82.2 %reduce-scatter.5.cloned.1.call-done = bf16[8,393216]{1,0:T(8,128)(2,1)} async-done(((bf16[32,393216]{1,0:T(8,128)(2,1)}), bf16[8,393216]{1,0:T(8,128)(2,1)}) %reduce-scatter.5.cloned.1.call-update) | async-done | bytes 6291472
  1309.1 21.1 fusion.59
  1334.7 10.1 convolution_bitcast_fusion.3
  1348.6 9.5 fusion.53
  1365.4 31.2 %all-reduce.17.cloned.1.call-done = (f32[2304]{0:T(1024)}, f32[3,3,384]{2,1,0:T(4,128)}, f32[1536]{0:T(1024)}, f32[3,3,1536]{2,1,0:T(4,128)}, f32[384]{0:T(512)}, /*index=5*/f32[768]{0:T(1024)}) async-done(((f32[2304]{0:T(1024)}, f32[3,3,384]{2,1,0:T(4,128)}, f32[1536]{0:T(1024)}, f32[3,3,1536]{2,1,0:T(4,128)}, f32[384]{0:T(512)}, /*index=5*/f32[768]{0:T(1024)}), (f32[2304]{0:T(1024)}, ...) | async-done | bytes 89104 | tf_op jit(solution)/shard_map/psum | solution.py:308
  1396.6 252.7 %all-reduce.19.cloned.1.call-done = (f32[256,2304]{1,0:T(8,128)}, f32[384,1152]{1,0:T(8,128)}, f32[384,384]{1,0:T(8,128)}, f32[384,1536]{1,0:T(8,128)}, f32[1536,384]{1,0:T(8,128)}, /*index=5*/f32[1536,768]{1,0:T(8,128)}) async-done(((f32[256,2304]{1,0:T(8,128)}, f32[384,1152]{1,0:T(8,128)}, f32[384,384]{1,0:T(8,128)}, f32[384,1536]{1,0:T(8,128)}, f32[1536,384]{1,0:T(8,128)}, ...) | async-done | bytes 14155792 | tf_op jit(solution)/shard_map/psum | solution.py:308
  1650.1 4.6 add_convert_fusion.3
  1654.7 22.8 %all_to_all.36 = bf16[16,4,16,768]{3,2,1,0:T(8,128)(2,1)S(1)} all-to-all(bf16[16,4,16,768]{3,2,1,0:T(8,128)(2,1)S(1)} %add_convert_fusion.3), channel_id=1, replica_groups=mesh['wide'=8,'narrow'=4] {'narrow'}, dimensions={0} | all-to-all | bytes 3145728 | tf_op jit(solution)/shard_map/all_to_all | solution.py:196
  1683.2 41.1 %all-reduce.13.cloned.1.call-done = (f32[2304]{0:T(1024)}, f32[3,3,384]{2,1,0:T(4,128)}, f32[1536]{0:T(1024)}, f32[3,3,1536]{2,1,0:T(4,128)}, f32[384]{0:T(512)}, /*index=5*/f32[768]{0:T(1024)}) async-done(((f32[2304]{0:T(1024)}, f32[3,3,384]{2,1,0:T(4,128)}, f32[1536]{0:T(1024)}, f32[3,3,1536]{2,1,0:T(4,128)}, f32[384]{0:T(512)}, /*index=5*/f32[768]{0:T(1024)}), (f32[2304]{0:T(1024)}, ...) | async-done | bytes 89104 | tf_op jit(solution)/shard_map/psum | solution.py:308
  1724.3 448.4 %all-reduce.15.cloned.1.call-done = (f32[256,2304]{1,0:T(8,128)}, f32[384,1152]{1,0:T(8,128)}, f32[384,384]{1,0:T(8,128)}, f32[384,1536]{1,0:T(8,128)}, f32[1536,384]{1,0:T(8,128)}, /*index=5*/f32[1536,768]{1,0:T(8,128)}) async-done(((f32[256,2304]{1,0:T(8,128)}, f32[384,1152]{1,0:T(8,128)}, f32[384,384]{1,0:T(8,128)}, f32[384,1536]{1,0:T(8,128)}, f32[1536,384]{1,0:T(8,128)}, ...) | async-done | bytes 14155792 | tf_op jit(solution)/shard_map/psum | solution.py:308
  (348 shorter events, 125.6 us)
Async XLA Ops:
  7.2 468.1 %copy-start = (bf16[1536,768]{1,0:T(8,128)(2,1)S(1)}, bf16[1536,768]{1,0:T(8,128)(2,1)}, u32[]{:S(2)}) copy-start(bf16[1536,768]{1,0:T(8,128)(2,1)} %param.28) | copy-start | bytes 7077892
  7.2 212.1 %all-gather.2.cloned.1.call-start = ((), (), s32[]{:S(2)}) async-start(), calls=%async_computation.3 | async-start | bytes 31457280 | tf_op jit(solution)/shard_map/all_gather | solution.py:164
  7.2 9.1 copy-start.1
  11.9 10.2 copy-start.65
  14.8 14.2 copy-start.30
  15.0 14.1 copy-start.54
  15.0 14.1 copy-start.56
  16.3 12.7 copy-start.32
  18.2 19.0 copy-start.8
  18.4 3.8 collective-permute-start
  20.8 5.7 collective-permute-start.1
  22.1 15.2 copy-start.66
  22.1 15.2 copy-start.68
  22.1 15.2 copy-start.70
  22.1 15.2 copy-start.72
  22.2 15.2 copy-start.74
  22.2 15.2 copy-start.76
  22.2 15.2 copy-start.78
  22.2 15.2 copy-start.80
  22.2 15.2 copy-start.82
  22.2 15.1 copy-start.21
  26.5 10.9 copy-start.23
  29.1 10.0 copy-start.102
  51.8 10.2 copy-start.94
  54.6 419.1 %all-to-all-start.1 = ((bf16[4,16,16,768]{3,2,0,1:T(8,128)(2,1)}), bf16[4,16,16,768]{3,2,0,1:T(8,128)(2,1)}, u32[]{:S(2)}, u32[]{:S(2)}) async-start(bf16[4,16,16,768]{3,2,0,1:T(8,128)(2,1)} %copy.92), calls=%async_computation.1 | async-start | bytes 3145728 | tf_op jit(solution)/shard_map/all_to_all | solution.py:197
  61.8 1239.6 %reduce-scatter.5.cloned.1.call-start = ((), (), s32[]{:S(2)}) async-start(), calls=%async_computation.4 | async-start | bytes 31457280
  335.3 58.1 %copy-start.14 = (f32[16,4,6,64]{3,2,1,0:T(8,128)}, f32[16,4,6,64]{3,2,1,0:T(8,128)S(1)}, u32[]{:S(2)}) copy-start(f32[16,4,6,64]{3,2,1,0:T(8,128)S(1)} %log_add_fusion) | copy-start | bytes 294916
  430.8 11.6 copy-start.28
  430.8 11.6 copy-start.45
  450.7 11.6 copy-start.34
  452.1 10.2 copy-start.42
  468.9 29.4 %collective-permute-start.2 = (bf16[16,1,32,1536]{3,2,1,0:T(8,128)(2,1)}, bf16[16,1,32,1536]{3,2,1,0:T(8,128)(2,1)}, u32[]{:S(2)}, u32[]{:S(2)}) collective-permute-start(bf16[16,1,32,1536]{3,2,1,0:T(8,128)(2,1)} %get-tuple-element.98), channel_id=1, source_target_pairs={{0,1},{1,2},{2,3},{4,5},{5,6},{6,7},{8,9},{9,10},{10,11},{12,13},{... | collective-permute-start | bytes 4718600 | tf_op jit(solution)/shard_map/ppermute | solution.py:17
  472.2 26.1 %collective-permute-start.3 = (bf16[16,1,32,1536]{3,2,1,0:T(8,128)(2,1)}, bf16[16,1,32,1536]{3,2,1,0:T(8,128)(2,1)}, u32[]{:S(2)}, u32[]{:S(2)}) collective-permute-start(bf16[16,1,32,1536]{3,2,1,0:T(8,128)(2,1)} %get-tuple-element.99), channel_id=1, source_target_pairs={{1,0},{2,1},{3,2},{5,4},{6,5},{7,6},{9,8},{10,9},{11,10},{13,12},{... | collective-permute-start | bytes 4718600 | tf_op jit(solution)/shard_map/ppermute | solution.py:20
  513.4 52.4 %copy-start.100 = (bf16[1536,384]{1,0:T(8,128)(2,1)S(1)}, bf16[1536,384]{1,0:T(8,128)(2,1)}, u32[]{:S(2)}) copy-start(bf16[1536,384]{1,0:T(8,128)(2,1)} %param.26) | copy-start | bytes 3538948
  632.6 6.0 collective-permute-start.4
  635.7 5.3 collective-permute-start.5
  661.7 50.8 %copy-start.35 = (f32[16,8,32]{2,1,0:T(8,128)S(1)}, f32[16,8,32]{2,1,0:T(8,128)}, u32[]{:S(2)}) copy-start(f32[16,8,32]{2,1,0:T(8,128)} %copy-done.34) | copy-start | bytes 49156
  661.7 50.8 %copy-start.49 = (f32[16,384]{1,0:T(8,128)S(1)}, f32[16,384]{1,0:T(8,128)}, u32[]{:S(2)}) copy-start(f32[16,384]{1,0:T(8,128)} %get-tuple-element.110) | copy-start | bytes 73732
  712.5 11.4 copy-start.38
  712.5 11.4 copy-start.43
  730.2 22.7 %copy-start.29 = (bf16[384,384]{1,0:T(8,128)(2,1)S(1)}, bf16[384,384]{1,0:T(8,128)(2,1)}, u32[]{:S(2)}) copy-start(bf16[384,384]{1,0:T(8,128)(2,1)} %param.22) | copy-start | bytes 884740
  730.2 22.7 %copy-start.46 = (f32[16,384]{1,0:T(8,128)S(1)}, f32[16,384]{1,0:T(8,128)}, u32[]{:S(2)}) copy-start(f32[16,384]{1,0:T(8,128)} %get-tuple-element.113) | copy-start | bytes 73732
  1104.1 292.5 %all-reduce.17.cloned.1.call-start = ((), (), s32[]{:S(2)}) async-start(), calls=%async_computation.7 | async-start | bytes 237568 | tf_op jit(solution)/shard_map/psum | solution.py:308
  1183.5 15.4 copy-start.47
  1198.9 11.4 slice-start
  1199.0 11.4 slice-start.6
  1331.4 14.4 collective-permute-start.6
  1333.2 12.6 copy-start.12
  1333.2 12.6 collective-permute-start.7
  1348.6 9.6 copy-start.40
  1348.6 9.6 copy-start.31
  1362.7 286.7 %all-reduce.19.cloned.1.call-start = ((), (), s32[]{:S(2)}) async-start(), calls=%async_computation.8 | async-start | bytes 28311552 | tf_op jit(solution)/shard_map/psum | solution.py:308
  1365.4 358.9 %all-reduce.13.cloned.1.call-start = ((), (), s32[]{:S(2)}) async-start(), calls=%async_computation.5 | async-start | bytes 237568 | tf_op jit(solution)/shard_map/psum | solution.py:308
  1396.6 776.1 %all-reduce.15.cloned.1.call-start = ((), (), s32[]{:S(2)}) async-start(), calls=%async_computation.6 | async-start | bytes 28311552 | tf_op jit(solution)/shard_map/psum | solution.py:308
  1650.1 28.7 %slice-start.2 = ((s8[6291456]{0:T(1024)(128)(4,1)}), s8[4194304]{0:T(1024)(128)(4,1)S(1)}, s32[]{:S(2)}) async-start(s8[6291456]{0:T(1024)(128)(4,1)} %bitcast.184), calls=%async_computation.11 | async-start | bytes 8388608
  1650.1 28.7 %slice-start.4 = ((s8[6291456]{0:T(1024)(128)(4,1)}), s8[4194304]{0:T(1024)(128)(4,1)S(1)}, s32[]{:S(2)}) async-start(s8[6291456]{0:T(1024)(128)(4,1)} %bitcast.193), calls=%async_computation.13 | async-start | bytes 8388608
  1650.1 28.7 %slice-start.3 = ((s8[6291456]{0:T(1024)(128)(4,1)}), s8[2097152]{0:T(1024)(128)(4,1)S(1)}, s32[]{:S(2)}) async-start(s8[6291456]{0:T(1024)(128)(4,1)} %bitcast.184), calls=%async_computation.12 | async-start | bytes 4194304
  1650.1 28.7 %slice-start.5 = ((s8[6291456]{0:T(1024)(128)(4,1)}), s8[2097152]{0:T(1024)(128)(4,1)S(1)}, s32[]{:S(2)}) async-start(s8[6291456]{0:T(1024)(128)(4,1)} %bitcast.193), calls=%async_computation.14 | async-start | bytes 4194304
  1654.7 24.1 %copy-start.3 = (bf16[16,8,32,384]{3,2,1,0:T(8,128)(2,1)S(1)}, bf16[16,8,32,384]{3,2,1,0:T(8,128)(2,1)}, u32[]{:S(2)}) copy-start(bf16[16,8,32,384]{3,2,1,0:T(8,128)(2,1)} %param.15) | copy-start | bytes 9437188
  2172.7 9.0 copy-start.41
  2172.7 9.8 copy-start.20
  2172.7 11.2 copy-start.93
  2172.7 11.8 copy-start.58
  2172.7 12.4 copy-start.19
  (65 other events, 277.7 us)
Sparse Core Ops, SparseCore 0:
  52.0 167.2 all-gather.1
  1104.2 197.1 reduce-scatter.4
  1362.8 33.6 all-reduce.16
  1400.7 248.6 all-reduce.18
  1653.3 70.8 all-reduce.12
  1730.3 442.2 all-reduce.14
